TPU v7x, 32 devices: a whole 2x2x4 slice. The times are simulated.
32 devices in a mesh: dp: 8 (over z, x), mp: 4 (over y, core).
Axes of the slice: x: 2, y: 2, z: 4, core: 2. Of those that a mesh axis runs over, the one named last changes fastest.
Arguments:
- inputs: bfloat16 [16384, 768], P('dp'), may hold values from -6 to 6
- segments: int32 [256, 64], P('dp'), may hold values from 0 to 5, never falling along the last dimension, each value on 1 to 24 neighbouring positions
- cotangent: bfloat16 [16384, 768], P('dp'), may hold values from -12 to 12
- triple_weight: float32 [3, 768, 768], P(None, 'dp', 'mp'), may hold values from -0.21875 to 0.21875
- triple_first: float32 [3, 768, 768], P(None, 'dp', 'mp')
- triple_second: float32 [3, 768, 768], P(None, 'dp', 'mp'), as said below
- outward_weight: float32 [768, 768], P('mp', 'dp'), may hold values from -0.625 to 0.625
- outward_first: float32 [768, 768], P('mp', 'dp')
- outward_second: float32 [768, 768], P('mp', 'dp'), as said below
- expand_weight: float32 [768, 3072], P('dp', 'mp'), may hold values from -2 to 2
- expand_first: float32 [768, 3072], P('dp', 'mp')
- expand_second: float32 [768, 3072], P('dp', 'mp'), as said below
- reduce_weight: float32 [3072, 768], P('mp', 'dp'), may hold values from -0.109375 to 0.109375
- reduce_first: float32 [3072, 768], P('mp', 'dp')
- reduce_second: float32 [3072, 768], P('mp', 'dp'), as said below
- norm_params: float32 [6, 768], replicated, may hold values from -3 to 4
- norm_first: float32 [6, 768], replicated
- norm_second: float32 [6, 768], replicated, as said below
- paired_bias: float32 [2, 768], P(None, 'mp'), may hold values from -1.8 to 1.8
- paired_first: float32 [2, 768], P(None, 'mp')
- paired_second: float32 [2, 768], P(None, 'mp'), as said below
- hidden_bias: float32 [3072], P('mp'), may hold values from -1.8 to 1.8
- hidden_first: float32 [3072], P('mp')
- hidden_second: float32 [3072], P('mp'), as said below
Outputs:
- outputs: bfloat16 [16384, 768], P('dp')
- input_gradient: bfloat16 [16384, 768], P('dp')
- gradient_norm: float32 [], replicated
- triple_moment: float32 [3, 768, 768], P(None, 'dp', 'mp')
- triple_square: float32 [3, 768, 768], P(None, 'dp', 'mp')
- triple_updated: float32 [3, 768, 768], P(None, 'dp', 'mp')
- outward_moment: float32 [768, 768], P('mp', 'dp')
- outward_square: float32 [768, 768], P('mp', 'dp')
- outward_updated: float32 [768, 768], P('mp', 'dp')
- expand_moment: float32 [768, 3072], P('dp', 'mp')
- expand_square: float32 [768, 3072], P('dp', 'mp')
- expand_updated: float32 [768, 3072], P('dp', 'mp')
- reduce_moment: float32 [3072, 768], P('mp', 'dp')
- reduce_square: float32 [3072, 768], P('mp', 'dp')
- reduce_updated: float32 [3072, 768], P('mp', 'dp')
- norm_moment: float32 [6, 768], replicated
- norm_square: float32 [6, 768], replicated
- norm_updated: float32 [6, 768], replicated
- paired_moment: float32 [2, 768], P(None, 'mp')
- paired_square: float32 [2, 768], P(None, 'mp')
- paired_updated: float32 [2, 768], P(None, 'mp')
- hidden_moment: float32 [3072], P('mp')
- hidden_square: float32 [3072], P('mp')
- hidden_updated: float32 [3072], P('mp')
Inputs may be any that keep to these rules, and one draw needn't show every extreme that they name: `segments`: within each row of 64 tokens the numbers never fall; each of the 6 captions holds 1 to 24 tokens, one exactly 24. `triple_second`: positive. `outward_second`: positive. `expand_second`: positive. `reduce_second`: positive. `norm_second`: positive. `paired_second`: positive. `hidden_second`: positive.
All inputs are finite; a program needn't handle non-finite values.
Results may differ from a plain program's by a relative error of at most 0.02.
Values may be sent and summed in bfloat16 or wider, within the bound.
No kernel may reach another device: no remote copies, remote signals or barrier semaphores. Data moves between devices by JAX's collectives and lax.ppermute only.
A program may use at most 128 MiB of HBM per device.

v0:
```python
import jax
import jax.numpy as jnp
from jax import lax
from jax.sharding import PartitionSpec as P

HD = 64
STEP = 5
EPS_NORM = 1e-06
BETA = 0.5
LR_MATRIX = 0.03
LR_VECTOR = 0.2
DECAY = 0.1
ADAM_EPS = 1e-08
CLIP = 1.0
NEG = -1e30


def norm_forward(rows_in, gain_row, shift_row):
    row_mean = jnp.mean(rows_in, axis=-1, keepdims=True)
    centred = rows_in - row_mean
    variance = jnp.mean(centred * centred, axis=-1, keepdims=True)
    scaled = lax.rsqrt(variance + EPS_NORM)
    normal_rows = centred * scaled
    return (normal_rows * gain_row + shift_row, normal_rows, scaled)


def norm_backward(upstream, normal_rows, scaled, gain_row):
    gained = upstream * gain_row
    mean_one = jnp.mean(gained, axis=-1, keepdims=True)
    mean_two = jnp.mean(gained * normal_rows, axis=-1, keepdims=True)
    return scaled * (gained - mean_one - normal_rows * mean_two)


def smooth_gate(values_in):
    return jax.nn.gelu(values_in, approximate=True)


def adam_step(weight, first, second, grad, factor, rate, decay):
    clipped = grad * factor
    first_new = BETA * first + (1.0 - BETA) * clipped
    second_new = BETA * second + (1.0 - BETA) * clipped * clipped
    correction = 1.0 - BETA**STEP
    direction = first_new / correction / (jnp.sqrt(second_new / correction) + ADAM_EPS)
    return (first_new, second_new, weight - rate * (direction + decay * weight))


def per_device(
    inputs,
    segments,
    cotangent,
    triple_weight,
    triple_first,
    triple_second,
    outward_weight,
    outward_first,
    outward_second,
    expand_weight,
    expand_first,
    expand_second,
    reduce_weight,
    reduce_first,
    reduce_second,
    norm_params,
    norm_first,
    norm_second,
    paired_bias,
    paired_first,
    paired_second,
    hidden_bias,
    hidden_first,
    hidden_second,
):
    f32 = jnp.float32
    bf16 = jnp.bfloat16
    dp_count = lax.axis_size("dp")
    mp_count = lax.axis_size("mp")
    triple_full, outward_full, expand_full, reduce_full = (
        lax.all_gather(triple_weight.astype(bf16), "dp", axis=1, tiled=True),
        lax.all_gather(outward_weight.astype(bf16), "dp", axis=1, tiled=True),
        lax.all_gather(expand_weight.astype(bf16), "dp", axis=0, tiled=True),
        lax.all_gather(reduce_weight.astype(bf16), "dp", axis=1, tiled=True),
    )
    row_count, row_length = segments.shape
    token_count = inputs.shape[0]
    head_width = triple_full.shape[2]
    head_count = head_width // HD
    scale_factor = HD ** (-0.5)
    grid = (row_count, row_length, head_count, HD)
    x_full = inputs.astype(f32)
    normed_one, normal_one, scaled_one = norm_forward(x_full, norm_params[0], norm_params[1])
    first_low = normed_one.astype(bf16)
    projected = jnp.einsum("td,cdw->ctw", first_low, triple_full, preferred_element_type=f32)
    queries = (projected[0] + paired_bias[0]).astype(bf16).reshape(grid)
    key_rows = projected[1].astype(bf16).reshape(grid)
    value_rows = (projected[2] + paired_bias[1]).astype(bf16).reshape(grid)
    same_caption = (segments[:, :, None] == segments[:, None, :])[:, None, :, :]

    def scores_of(query_in, key_in):
        raw_scores = jnp.einsum("rqhd,rkhd->rhqk", query_in, key_in, preferred_element_type=f32)
        return jnp.where(same_caption, raw_scores * scale_factor, NEG)

    scores = scores_of(queries, key_rows)
    row_top = jnp.max(scores, axis=-1, keepdims=True)
    lifted = jnp.exp(scores - row_top)
    row_total = jnp.sum(lifted, axis=-1, keepdims=True)
    probs = lifted / row_total
    log_total = row_top + jnp.log(row_total)
    context = jnp.einsum(
        "rhqk,rkhd->rqhd", probs.astype(bf16), value_rows, preferred_element_type=f32
    )
    context_low = context.astype(bf16).reshape(token_count, head_width)
    attn_part = jnp.dot(context_low, outward_full, preferred_element_type=f32)
    attended = lax.psum(attn_part.astype(jnp.bfloat16), "mp").astype(jnp.float32)
    middle = x_full + attended + norm_params[4]
    normed_two, normal_two, scaled_two = norm_forward(middle, norm_params[2], norm_params[3])
    second_low = normed_two.astype(bf16)
    hidden_pre = jnp.dot(second_low, expand_full, preferred_element_type=f32) + hidden_bias
    gate_out, gelu_pull = jax.vjp(smooth_gate, hidden_pre)
    activated = gate_out.astype(bf16)
    fed_part = jnp.dot(activated, reduce_full, preferred_element_type=f32)
    fed = lax.psum(fed_part.astype(jnp.bfloat16), "mp").astype(jnp.float32)
    outputs = (middle + fed + norm_params[5]).astype(bf16)
    cot_full = cotangent.astype(f32)
    grad_reduce = jnp.einsum("tf,td->fd", activated, cotangent, preferred_element_type=f32)
    act_grad = jnp.einsum("td,fd->tf", cotangent, reduce_full, preferred_element_type=f32)
    hidden_grad = gelu_pull(act_grad)[0].astype(bf16)
    grad_expand = jnp.einsum("td,tf->df", second_low, hidden_grad, preferred_element_type=f32)
    grad_hidden = jnp.sum(hidden_grad, axis=0, dtype=f32)
    second_part = jnp.einsum("tf,df->td", hidden_grad, expand_full, preferred_element_type=f32)
    second_grad = lax.psum(second_part.astype(jnp.bfloat16), "mp").astype(jnp.float32)
    middle_grad = cot_full + norm_backward(second_grad, normal_two, scaled_two, norm_params[2])
    middle_low = middle_grad.astype(bf16)
    grad_outward = jnp.einsum("tw,td->wd", context_low, middle_low, preferred_element_type=f32)
    context_grad = (
        jnp.einsum("td,wd->tw", middle_low, outward_full, preferred_element_type=f32)
        .astype(bf16)
        .reshape(grid)
    )
    probs_again = jnp.exp(scores_of(queries, key_rows) - log_total)
    probs_low = probs_again.astype(bf16)
    value_grad = jnp.einsum(
        "rhqk,rqhd->rkhd", probs_low, context_grad, preferred_element_type=f32
    ).astype(bf16)
    prob_grad = jnp.einsum("rqhd,rkhd->rhqk", context_grad, value_rows, preferred_element_type=f32)
    inner = jnp.sum(prob_grad * probs_again, axis=-1, keepdims=True)
    score_grad = (probs_again * (prob_grad - inner) * scale_factor).astype(bf16)
    query_grad = jnp.einsum(
        "rhqk,rkhd->rqhd", score_grad, key_rows, preferred_element_type=f32
    ).astype(bf16)
    key_grad = jnp.einsum(
        "rhqk,rqhd->rkhd", score_grad, queries, preferred_element_type=f32
    ).astype(bf16)
    stacked = jnp.stack([query_grad, key_grad, value_grad]).reshape(3, token_count, head_width)
    grad_triple = jnp.einsum("td,ctw->cdw", first_low, stacked, preferred_element_type=f32)
    grad_paired = jnp.stack(
        [jnp.sum(stacked[0], axis=0, dtype=f32), jnp.sum(stacked[2], axis=0, dtype=f32)]
    )
    first_part = jnp.einsum("ctw,cdw->td", stacked, triple_full, preferred_element_type=f32)
    first_grad = lax.psum(first_part.astype(jnp.bfloat16), "mp").astype(jnp.float32)
    input_gradient = (
        middle_grad + norm_backward(first_grad, normal_one, scaled_one, norm_params[0])
    ).astype(bf16)
    grad_norms = jnp.stack(
        [
            jnp.sum(first_grad * normal_one, axis=0),
            jnp.sum(first_grad, axis=0),
            jnp.sum(second_grad * normal_two, axis=0),
            jnp.sum(second_grad, axis=0),
            jnp.sum(middle_grad, axis=0),
            jnp.sum(cot_full, axis=0),
        ]
    )
    owned = (
        lax.psum_scatter(grad_triple, "dp", scatter_dimension=1, tiled=True),
        lax.psum_scatter(grad_outward, "dp", scatter_dimension=1, tiled=True),
        lax.psum_scatter(grad_expand, "dp", scatter_dimension=0, tiled=True),
        lax.psum_scatter(grad_reduce, "dp", scatter_dimension=1, tiled=True),
    )
    vectors = lax.psum((grad_norms, grad_paired, grad_hidden), "dp")
    local_square = jnp.zeros((), f32)
    for grad_item in owned:
        local_square = local_square + jnp.sum(grad_item * grad_item)
    local_square = local_square + jnp.sum(vectors[0] * vectors[0]) / (dp_count * mp_count)
    local_square = (
        local_square
        + (jnp.sum(vectors[1] * vectors[1]) + jnp.sum(vectors[2] * vectors[2])) / dp_count
    )
    total_square = lax.psum(local_square, ("dp", "mp"))
    gradient_norm = jnp.sqrt(total_square)
    factor = jnp.minimum(1.0, CLIP / gradient_norm)
    triple_new = adam_step(
        triple_weight, triple_first, triple_second, owned[0], factor, LR_MATRIX, DECAY
    )
    outward_new = adam_step(
        outward_weight, outward_first, outward_second, owned[1], factor, LR_MATRIX, DECAY
    )
    expand_new = adam_step(
        expand_weight, expand_first, expand_second, owned[2], factor, LR_MATRIX, DECAY
    )
    reduce_new = adam_step(
        reduce_weight, reduce_first, reduce_second, owned[3], factor, LR_MATRIX, DECAY
    )
    norm_new = adam_step(norm_params, norm_first, norm_second, vectors[0], factor, LR_VECTOR, 0.0)
    paired_new = adam_step(
        paired_bias, paired_first, paired_second, vectors[1], factor, LR_VECTOR, 0.0
    )
    hidden_new = adam_step(
        hidden_bias, hidden_first, hidden_second, vectors[2], factor, LR_VECTOR, 0.0
    )
    return (
        outputs,
        input_gradient,
        gradient_norm,
        triple_new[0],
        triple_new[1],
        triple_new[2],
        outward_new[0],
        outward_new[1],
        outward_new[2],
        expand_new[0],
        expand_new[1],
        expand_new[2],
        reduce_new[0],
        reduce_new[1],
        reduce_new[2],
        norm_new[0],
        norm_new[1],
        norm_new[2],
        paired_new[0],
        paired_new[1],
        paired_new[2],
        hidden_new[0],
        hidden_new[1],
        hidden_new[2],
    )


def solution(mesh):
    placed = (
        P("dp", None),
        P("dp", None),
        P("dp", None),
        P(None, "dp", "mp"),
        P(None, "dp", "mp"),
        P(None, "dp", "mp"),
        P("mp", "dp"),
        P("mp", "dp"),
        P("mp", "dp"),
        P("dp", "mp"),
        P("dp", "mp"),
        P("dp", "mp"),
        P("mp", "dp"),
        P("mp", "dp"),
        P("mp", "dp"),
        P(),
        P(),
        P(),
        P(None, "mp"),
        P(None, "mp"),
        P(None, "mp"),
        P("mp"),
        P("mp"),
        P("mp"),
    )
    return jax.shard_map(
        per_device,
        mesh=mesh,
        in_specs=placed,
        out_specs=(
            P("dp", None),
            P("dp", None),
            P(),
            P(None, "dp", "mp"),
            P(None, "dp", "mp"),
            P(None, "dp", "mp"),
            P("mp", "dp"),
            P("mp", "dp"),
            P("mp", "dp"),
            P("dp", "mp"),
            P("dp", "mp"),
            P("dp", "mp"),
            P("mp", "dp"),
            P("mp", "dp"),
            P("mp", "dp"),
            P(),
            P(),
            P(),
            P(None, "mp"),
            P(None, "mp"),
            P(None, "mp"),
            P("mp"),
            P("mp"),
            P("mp"),
        ),
        check_vma=False,
    )
```

profile of v0, /device:TPU:0, one launch (start us, length us, event | category | flops | bytes accessed | tf_op | source)
XLA Modules:
  0.0 715.4 jit_solution(5087993690982692376)
XLA Ops:
  8.1 2.5 convert_reduce_fusion.2
  12.8 40.5 %all_gather.12 = bf16[3,768,192]{2,0,1:T(4,128)(2,1)} all-gather(bf16[3,96,192]{2,0,1:T(4,128)(2,1)S(1)} %copy.118), channel_id=1, replica_groups=mesh['dp'=8,'mp'=4] {'dp'}, dimensions={1}, use_global_device_ids=true | all-gather | bytes 995328 | tf_op jit(solution)/shard_map/all_gather | solution.py:78
  53.2 3.4 copy.119
  56.7 3.4 fusion.96
  61.1 2.0 fusion.107
  65.1 31.9 %all_gather.13 = bf16[192,768]{0,1:T(8,128)(2,1)S(1)} all-gather(bf16[192,96]{0,1:T(8,128)(2,1)} %copy.127), channel_id=1, replica_groups=mesh['dp'=8,'mp'=4] {'dp'}, dimensions={1}, use_global_device_ids=true | all-gather | bytes 331776 | tf_op jit(solution)/shard_map/all_gather | solution.py:79
  97.0 3.4 convert_element_type.130
  100.4 3.4 copy.123
  103.8 3.6 squeeze.4
  107.4 3.9 copy.120
  111.3 3.6 squeeze.10
  114.9 5.7 fusion.108
  121.5 2.1 copy-done.5
  124.7 2.2 copy.126
  126.9 3.5 reshape.145
  130.4 3.9 convolution_convert_fusion.2
  138.0 63.8 %all-reduce.6.cloned.1.call-done = bf16[2048,768]{1,0:T(8,128)(2,1)} async-done(((bf16[2048,768]{1,0:T(8,128)(2,1)}), bf16[2048,768]{1,0:T(8,128)(2,1)}) %all-reduce.6.cloned.1.call-update) | async-done | bytes 3145744 | tf_op jit(solution)/shard_map/psum | solution.py:113
  201.8 3.1 fusion.46
  205.0 1.8 multiply_reduce_fusion
  207.4 3.0 add_convert_fusion.1
  210.4 7.5 %fusion.111 = f32[2048,768]{1,0:T(8,128)} fusion(bf16[2048,768]{1,0:T(8,128)(2,1)} %add_convert_fusion.1, bf16[768,768]{1,0:T(8,128)(2,1)} %all-gather.3.cloned.1.call-done), kind=kOutput, calls=%fused_computation.161 | convolution fusion | flops 2415919104 | bytes 10616832 | tf_op jit(solution)/shard_map/dot_general | solution.py:117
  217.9 2.4 all-gather.5.cloned.1.call-done
  220.3 10.8 %convert_reduce_fusion.4 = (f32[768]{0:T(1024)}, bf16[2048,768]{1,0:T(8,128)(2,1)S(1)}, bf16[2048,768]{1,0:T(8,128)(2,1)}) fusion(f32[2048,768]{1,0:T(8,128)} %fusion.111, f32[768]{0:T(1024)} %param.45, bf16[2048,768]{1,0:T(8,128)(2,1)} %param.26, bf16[768,768]{0,1:T(8,128)(2,1)} %all-gather.5.cloned.1.call-done), kind=kOutput, calls=%fused_computation.46 | convolution fusion | flops 2455239936 | bytes 16914432 | tf_op jit(solution)/shard_map/td,fd->tf/dot_general | solution.py:125
  231.1 1.7 copy-done.57
  232.8 4.0 convolution_convert_fusion
  238.7 6.6 convolution_convert_fusion.1
  245.2 58.7 %all-reduce.8.cloned.1.call-done = bf16[2048,768]{1,0:T(8,128)(2,1)} async-done(((bf16[2048,768]{1,0:T(8,128)(2,1)}), bf16[2048,768]{1,0:T(8,128)(2,1)}) %all-reduce.8.cloned.1.call-update) | async-done | bytes 3145744 | tf_op jit(solution)/shard_map/psum | solution.py:130
  303.9 7.1 fusion.30
  311.1 4.7 fusion.106
  315.8 2.7 copy-done.3
  318.5 2.3 fusion.78
  320.7 4.9 convolution_convert_fusion.3
  325.6 3.4 reshape.146
  329.0 3.6 copy.128
  332.7 5.1 fusion.81
  337.8 10.3 %fusion.71 = bf16[32,64,3,64]{1,3,2,0:T(8,128)(2,1)} fusion(f32[32,3,64,64]{2,3,1,0:T(8,128)} %fusion.81, f32[32,3,64,64]{2,3,1,0:T(8,128)} %copy-done.4, f32[32,3,64]{2,1,0:T(4,128)S(1)} %copy-done.23, f32[32,64,3,64]{1,0,3,2:T(8,128)} %squeeze.10, f32[3,64]{1,0:T(4,128)S(1)} %copy-done.47), kind=kOutput, calls=%fused_computation.91 | convolution fusion | flops 54270016 | bytes 5530368 | tf_op jit(solution)/shard_map/rhqk,rqhd->rkhd/dot_general | solution.py:150
  348.1 8.1 %convert_reduce_fusion.6 = (f32[3,64]{1,0:T(4,128)S(1)}, bf16[32,64,3,64]{3,1,2,0:T(8,128)(2,1)}) fusion(bf16[32,64,3,64]{3,1,2,0:T(8,128)(2,1)} %copy.123, f32[32,3,64,64]{2,3,1,0:T(8,128)} %fusion.81, f32[32,3,64,64]{2,3,1,0:T(8,128)} %copy-done.4, f32[32,3,64]{2,1,0:T(4,128)S(1)} %copy-done.23), kind=kOutput, calls=%fused_computation.60 | convolution fusion | flops 54269824 | bytes 4743936 | tf_op jit(solution)/shard_map/rhqk,rkhd->rqhd/dot_general | solution.py:147
  356.2 4.4 convert_reduce_fusion.5
  360.6 3.6 copy.131
  364.2 3.5 stack.42
  367.8 2.1 constant_dynamic-update-slice_fusion.2
  369.9 3.6 copy.133
  373.4 3.5 stack.43
  377.0 3.2 copy.135
  380.1 3.5 stack.44
  383.7 2.2 constant_dynamic-update-slice_fusion.1
  385.8 2.1 constant_dynamic-update-slice_fusion
  387.9 6.0 bitcast_convert_fusion
  394.0 7.1 fusion.112
  401.4 6.9 fusion.113
  408.4 5.2 fusion.65
  413.6 4.2 copy.149
  417.8 4.7 reshape.151
  423.4 1.8 copy.137
  425.3 1.8 copy.138
  429.0 85.0 %all-reduce.10.cloned.1.call-done = (bf16[2048,768]{1,0:T(8,128)(2,1)}, bf16[2048,768]{1,0:T(8,128)(2,1)}) async-done(((bf16[2048,768]{1,0:T(8,128)(2,1)}, bf16[2048,768]{1,0:T(8,128)(2,1)}), (bf16[2048,768]{1,0:T(8,128)(2,1)}, bf16[2048,768]{1,0:T(8,128)(2,1)})) %all-reduce.10.cloned.1.call-update) | async-done | bytes 6291472 | tf_op jit(solution)/shard_map/psum | solution.py:121
  514.0 4.6 fusion.31
  518.7 37.3 %all-reduce = (f32[6,768]{1,0:T(8,128)S(1)}, f32[2,192]{1,0:T(2,128)S(1)}, f32[768]{0:T(1024)S(1)}) all-reduce(f32[6,768]{1,0:T(8,128)S(1)} %stack.52, f32[2,192]{1,0:T(2,128)S(1)} %pad_maximum_fusion, f32[768]{0:T(1024)S(1)} %copy-done.53), channel_id=1, replica_groups=mesh['dp'=8,'mp'=4] {'dp'}, use_global_device_ids=true, to_apply=%region_29.30 | all-reduce | flops 5760 | bytes 46080 | tf_op jit(solution)/shard_map/psum | solution.py:179
  559.8 1.6 multiply_reduce_fusion.3
  561.4 6.3 reduce-scatter.11.cloned.1.call-done
  570.5 67.2 %reduce-scatter.13.cloned.1.call-done = f32[96,576]{1,0:T(8,128)} async-done(((f32[768,576]{1,0:T(8,128)}), f32[96,576]{1,0:T(8,128)}) %reduce-scatter.13.cloned.1.call-update) | async-done | bytes 221200
  637.7 1.9 reshape.152
  644.0 10.6 %fusion.16 = (bf16[2048,768]{1,0:T(8,128)(2,1)}, bf16[2048,768]{1,0:T(8,128)(2,1)}) fusion(f32[2048,768]{1,0:T(8,128)} %copy-done.3, bf16[2048,768]{1,0:T(8,128)(2,1)S(1)} %copy-done, bf16[2048,768]{1,0:T(8,128)(2,1)} %get-tuple-element.140, f32[2048]{0:T(1024)} %broadcast_multiply_fusion, f32[2048]{0:T(1024)} %broadcast_multiply_fusion.1, ...), kind=kLoop, calls=%fused_computation.29 | loop fusion | flops 28311552 | bytes 25207808 | tf_op jit(solution)/shard_map/convert_element_type | solution.py:162
  654.7 39.5 %psum.63 = f32[]{:T(128)} all-reduce(f32[]{:T(128)S(6)} %add.294), channel_id=1, replica_groups=mesh['dp'=8,'mp'=4] {'dp','mp'}, use_global_device_ids=true, to_apply=%region_38.39 | all-reduce | flops 1 | bytes 8 | tf_op jit(solution)/shard_map/psum | solution.py:188
  (185 shorter events, 34.8 us)
Async XLA Ops:
  8.0 2.8 copy-start
  8.0 3.9 copy-start.31
  8.0 4.5 copy-start.13
  8.1 193.7 %all-reduce.6.cloned.1.call-start = ((), (), s32[]{:S(2)}) async-start(), calls=%async_computation.4 | async-start | bytes 6291456 | tf_op jit(solution)/shard_map/psum | solution.py:113
  10.9 45.8 %copy-start.25 = (f32[2048]{0:T(1024)}, f32[2048]{0:T(1024)S(1)}, u32[]{:S(2)}) copy-start(f32[2048]{0:T(1024)S(1)} %broadcast_multiply_fusion.5) | copy-start | bytes 24580
  12.0 48.1 %copy-start.32 = (f32[2048]{0:T(1024)}, f32[2048]{0:T(1024)S(1)}, u32[]{:S(2)}) copy-start(f32[2048]{0:T(1024)S(1)} %add_rsqrt_fusion.1) | copy-start | bytes 24580
  12.6 47.5 %copy-start.35 = (f32[768]{0:T(1024)}, f32[768]{0:T(1024)S(1)}, u32[]{:S(2)}) copy-start(f32[768]{0:T(1024)S(1)} %get-tuple-element.133) | copy-start | bytes 9220
  12.6 47.5 %copy-start.54 = (f32[768]{0:T(1024)}, f32[768]{0:T(1024)S(1)}, u32[]{:S(2)}) copy-start(f32[768]{0:T(1024)S(1)} %get-tuple-element.132) | copy-start | bytes 9220
  61.1 2.0 copy-start.50
  61.1 2.2 copy-start.17
  61.1 2.9 copy-start.34
  63.2 58.3 %copy-start.44 = (f32[3,64]{1,0:T(4,128)}, f32[3,64]{1,0:T(4,128)S(1)}, u32[]{:S(2)}) copy-start(f32[3,64]{1,0:T(4,128)S(1)} %add.264) | copy-start | bytes 2308
  63.3 51.6 %copy-start.46 = (f32[3,64]{1,0:T(4,128)}, f32[3,64]{1,0:T(4,128)S(1)}, u32[]{:S(2)}) copy-start(f32[3,64]{1,0:T(4,128)S(1)} %add.267) | copy-start | bytes 2308
  120.6 4.1 copy-start.4
  120.6 4.1 copy-start.16
  120.6 3.0 copy-start.5
  134.3 76.0 %all-gather.3.cloned.1.call-start = ((), (), s32[]{:S(2)}) async-start(), calls=%async_computation.5 | async-start | bytes 1327104 | tf_op jit(solution)/shard_map/all_gather | solution.py:80
  136.0 84.2 %all-gather.5.cloned.1.call-start = ((), (), s32[]{:S(2)}) async-start(), calls=%async_computation.6 | async-start | bytes 1327104 | tf_op jit(solution)/shard_map/all_gather | solution.py:81
  137.8 166.2 %all-reduce.8.cloned.1.call-start = ((), (), s32[]{:S(2)}) async-start(), calls=%async_computation.7 | async-start | bytes 6291456 | tf_op jit(solution)/shard_map/psum | solution.py:130
  201.8 3.2 copy-start.1
  205.0 2.4 copy-start.37
  220.3 12.5 %copy-start.56 = (bf16[768,768]{1,0:T(8,128)(2,1)S(1)}, bf16[768,768]{1,0:T(8,128)(2,1)}, u32[]{:S(2)}) copy-start(bf16[768,768]{1,0:T(8,128)(2,1)} %all-gather.3.cloned.1.call-done) | copy-start | bytes 3538948
  236.9 190.5 %reduce-scatter.15.cloned.1.call-start = ((), (), s32[]{:S(2)}) async-start(), calls=%async_computation.11 | async-start | bytes 884736
  303.9 7.1 copy-start.2
  303.9 7.1 copy-start.6
  303.9 7.1 copy-start.8
  303.9 7.1 copy-start.28
  311.0 7.4 %copy-start.7 = (bf16[2048,192]{0,1:T(8,128)(2,1)S(1)}, bf16[2048,192]{0,1:T(8,128)(2,1)}, u32[]{:S(2)}) copy-start(bf16[2048,192]{0,1:T(8,128)(2,1)} %reshape.145) | copy-start | bytes 2359300
  315.8 2.7 copy-start.3
  325.6 7.0 copy-start.45
  332.6 5.1 copy-start.23
  332.6 5.1 copy-start.47
  360.5 153.4 %all-reduce.10.cloned.1.call-start = ((), (), s32[]{:S(2)}) async-start(), calls=%async_computation.12 | async-start | bytes 12582912 | tf_op jit(solution)/shard_map/psum | solution.py:121
  383.7 4.3 copy-start.15
  394.0 165.8 %reduce-scatter.9.cloned.1.call-start = ((), (), s32[]{:S(2)}) async-start(), calls=%async_computation.8 | async-start | bytes 2654208 | tf_op jit(solution)/shard_map/reduce_scatter | solution.py:176
  401.1 7.3 %copy-start.26 = (f32[2048]{0:T(1024)S(1)}, f32[2048]{0:T(1024)}, u32[]{:S(2)}) copy-start(f32[2048]{0:T(1024)} %copy-done.25) | copy-start | bytes 24580
  401.1 7.3 %copy-start.33 = (f32[2048]{0:T(1024)S(1)}, f32[2048]{0:T(1024)}, u32[]{:S(2)}) copy-start(f32[2048]{0:T(1024)} %copy-done.32) | copy-start | bytes 24580
  401.1 7.3 %copy-start.36 = (f32[768]{0:T(1024)S(1)}, f32[768]{0:T(1024)}, u32[]{:S(2)}) copy-start(f32[768]{0:T(1024)} %copy-done.35) | copy-start | bytes 9220
  401.1 7.3 %copy-start.55 = (f32[768]{0:T(1024)S(1)}, f32[768]{0:T(1024)}, u32[]{:S(2)}) copy-start(f32[768]{0:T(1024)} %copy-done.54) | copy-start | bytes 9220
  401.1 166.6 %reduce-scatter.11.cloned.1.call-start = ((), (), s32[]{:S(2)}) async-start(), calls=%async_computation.9 | async-start | bytes 2654208 | tf_op jit(solution)/shard_map/reduce_scatter | solution.py:177
  408.3 229.4 %reduce-scatter.13.cloned.1.call-start = ((), (), s32[]{:S(2)}) async-start(), calls=%async_computation.10 | async-start | bytes 2211840
  417.8 4.8 copy-start.14
  422.5 4.6 copy-start.39
  422.5 4.6 copy-start.38
  422.5 4.6 copy-start.43
  422.5 4.6 copy-start.42
  514.0 4.7 copy-start.53
  556.0 83.6 %copy-start.30 = (f32[6,768]{1,0:T(8,128)}, f32[6,768]{1,0:T(8,128)S(1)}, u32[]{:S(2)}) copy-start(f32[6,768]{1,0:T(8,128)S(1)} %get-tuple-element.136) | copy-start | bytes 55300
  556.0 83.6 %copy-start.40 = (f32[768]{0:T(1024)}, f32[768]{0:T(1024)S(1)}, u32[]{:S(2)}) copy-start(f32[768]{0:T(1024)S(1)} %get-tuple-element.138) | copy-start | bytes 9220
  556.0 83.6 %copy-start.48 = (f32[2,192]{1,0:T(2,128)}, f32[2,192]{1,0:T(2,128)S(1)}, u32[]{:S(2)}) copy-start(f32[2,192]{1,0:T(2,128)S(1)} %get-tuple-element.137) | copy-start | bytes 4612
  654.6 44.5 %copy-start.49 = (f32[2,192]{1,0:T(2,128)S(1)}, f32[2,192]{1,0:T(2,128)}, u32[]{:S(2)}) copy-start(f32[2,192]{1,0:T(2,128)} %copy-done.48) | copy-start | bytes 4612
  654.6 44.5 %copy-start.51 = (f32[2,192]{1,0:T(2,128)S(1)}, f32[2,192]{1,0:T(2,128)}, u32[]{:S(2)}) copy-start(f32[2,192]{1,0:T(2,128)} %param.42) | copy-start | bytes 4612
  654.6 45.8 %copy-start.41 = (f32[768]{0:T(1024)S(1)}, f32[768]{0:T(1024)}, u32[]{:S(2)}) copy-start(f32[768]{0:T(1024)} %copy-done.40) | copy-start | bytes 9220
  654.6 45.8 %copy-start.52 = (f32[768]{0:T(1024)S(1)}, f32[768]{0:T(1024)}, u32[]{:S(2)}) copy-start(f32[768]{0:T(1024)} %param.45) | copy-start | bytes 9220
  654.7 48.5 %copy-start.18 = (f32[192,96]{1,0:T(8,128)S(1)}, f32[192,96]{1,0:T(8,128)}, u32[]{:S(2)}) copy-start(f32[192,96]{1,0:T(8,128)} %param.30) | copy-start | bytes 221188
  654.7 48.5 %copy-start.29 = (f32[192,96]{1,0:T(8,128)S(1)}, f32[192,96]{1,0:T(8,128)}, u32[]{:S(2)}) copy-start(f32[192,96]{1,0:T(8,128)} %param.32) | copy-start | bytes 221188
  654.7 50.1 %copy-start.9 = (f32[96,768]{1,0:T(8,128)S(1)}, f32[96,768]{1,0:T(8,128)}, u32[]{:S(2)}) copy-start(f32[96,768]{1,0:T(8,128)} %param.33) | copy-start | bytes 884740
  654.7 50.1 %copy-start.11 = (f32[96,768]{1,0:T(8,128)S(1)}, f32[96,768]{1,0:T(8,128)}, u32[]{:S(2)}) copy-start(f32[96,768]{1,0:T(8,128)} %reduce-scatter.9.cloned.1.call-done) | copy-start | bytes 884740
  654.7 50.1 %copy-start.19 = (f32[96,768]{1,0:T(8,128)S(1)}, f32[96,768]{1,0:T(8,128)}, u32[]{:S(2)}) copy-start(f32[96,768]{1,0:T(8,128)} %param.35) | copy-start | bytes 884740
  654.7 50.1 %copy-start.20 = (f32[96,768]{1,0:T(8,128)S(1)}, f32[96,768]{1,0:T(8,128)}, u32[]{:S(2)}) copy-start(f32[96,768]{1,0:T(8,128)} %param.34) | copy-start | bytes 884740
  695.0 10.9 %copy-start.10 = (f32[768,96]{0,1:T(8,128)S(1)}, f32[768,96]{0,1:T(8,128)}, u32[]{:S(2)}) copy-start(f32[768,96]{0,1:T(8,128)} %param.36) | copy-start | bytes 884740
  695.0 10.9 %copy-start.12 = (f32[768,96]{0,1:T(8,128)S(1)}, f32[768,96]{0,1:T(8,128)}, u32[]{:S(2)}) copy-start(f32[768,96]{0,1:T(8,128)} %reduce-scatter.11.cloned.1.call-done) | copy-start | bytes 884740
  695.0 10.9 %copy-start.21 = (f32[768,96]{0,1:T(8,128)S(1)}, f32[768,96]{0,1:T(8,128)}, u32[]{:S(2)}) copy-start(f32[768,96]{0,1:T(8,128)} %param.38) | copy-start | bytes 884740
  696.5 9.4 %copy-start.22 = (f32[768,96]{0,1:T(8,128)S(1)}, f32[768,96]{0,1:T(8,128)}, u32[]{:S(2)}) copy-start(f32[768,96]{0,1:T(8,128)} %param.37) | copy-start | bytes 884740
  (3 other events, 3.3 us)
Sparse Core Ops, SparseCore 0:
  134.4 67.2 all-reduce.5
  237.0 66.9 all-reduce.7
  394.1 119.8 all-reduce.9
Sparse Core Ops, SparseCore 1:
  137.6 40.2 all-gather.2
  180.5 39.8 all-gather.4
  360.6 62.6 reduce-scatter.14
  427.2 68.3 reduce-scatter.8
  499.5 68.2 reduce-scatter.10
  571.6 66.1 reduce-scatter.12
where the time goes:
time: 722 us; the launch traced here: 715 us
  waiting for transfers between devices  284 us (39%)
  blocking collectives  149 us (21%)
  matrix products  103 us (14%)
  local copies, waits for them, and re-layouts  94 us (13%)
  other arithmetic  62.2 us (9%)
  between operations  22.6 us (3%)
    psum x1, waiting for transfers between devices, per_device(): fed = lax.psum(fed_part.astype(jnp.bfloat16), 'mp').astype(jnp.float32)  85 us
    unnamed x11, waiting for transfers between devices  67.4 us
    psum x1, waiting for transfers between devices, per_device(): lax.psum(attn_part.astype(jnp.bfloat16), 'mp').astype(jnp.float32)  63.8 us
    psum x1, waiting for transfers between devices, per_device(): lax.psum(second_part.astype(jnp.bfloat16), 'mp').astype(jnp.float32)  58.7 us
    all_gather x1, blocking collectives, per_device(): lax.all_gather(triple_weight.astype(bf16), 'dp', axis=1, tiled=True)  40.5 us
    psum x1, blocking collectives, per_device(): total_square = lax.psum(local_square, ('dp', 'mp'))  39.5 us
    psum x1, blocking collectives, per_device(): vectors = lax.psum((grad_norms, grad_paired, grad_hidden), 'dp')  37.3 us
    unnamed x130, local copies, waits for them, and re-layouts  32.6 us
  transfers between devices with their start and end apart: 9, of which 6 were waited for; matrix products, arithmetic and copies ran while one was open for 15% of the time, Pallas kernels for 0%

commit v1 on v0

--- a/solution.py
+++ b/solution.py
@@ -70,6 +70,10 @@
     hidden_first,
     hidden_second,
 ):
+
+    def get_spans_here(tile_in):
+        return lax.all_gather(tile_in, axis_name="mp").sum(axis=0)
+
     f32 = jnp.float32
     bf16 = jnp.bfloat16
     dp_count = lax.axis_size("dp")
@@ -118,7 +122,7 @@
     gate_out, gelu_pull = jax.vjp(smooth_gate, hidden_pre)
     activated = gate_out.astype(bf16)
     fed_part = jnp.dot(activated, reduce_full, preferred_element_type=f32)
-    fed = lax.psum(fed_part.astype(jnp.bfloat16), "mp").astype(jnp.float32)
+    fed = get_spans_here(fed_part.astype(jnp.bfloat16)).astype(jnp.float32)
     outputs = (middle + fed + norm_params[5]).astype(bf16)
     cot_full = cotangent.astype(f32)
     grad_reduce = jnp.einsum("tf,td->fd", activated, cotangent, preferred_element_type=f32)

time: 722 us -> 677 us (0.938)
  waiting for transfers between devices: 284 us -> 232 us
  other arithmetic: 62.2 us -> 71 us
    all_gather x0 -> x1, waiting for transfers between devices: none -> 76.9 us  [get_spans_here(): return lax.all_gather(tile_in, axis_name='mp').sum(axis=0)]
    unnamed x11 -> x12, waiting for transfers between devices: 67.4 us -> 13 us
    psum x1, waiting for transfers between devices: 85 us -> 31.1 us  [per_device(): lax.psum(first_part.astype(jnp.bfloat16), 'mp').astype(jnp.float32)]
    psum x1, waiting for transfers between devices: 58.7 us -> 44.7 us  [per_device(): lax.psum(second_part.astype(jnp.bfloat16), 'mp').astype(jnp.float32)]
    reduce_sum x0 -> x1, other arithmetic: none -> 9.01 us  [get_spans_here(): return lax.all_gather(tile_in, axis_name='mp').sum(axis=0)]
    unnamed x130 -> x122, local copies, waits for them, and re-layouts: 32.6 us -> 33.4 us
  transfers between devices with their start and end apart: 9 -> 10, of which waited for: 6 -> 6; matrix products, arithmetic and copies ran while one was open for 15% -> 26% of each run, Pallas kernels for 0% -> 0%
where the time goes in v1:
time: 677 us; the launch traced here: 670 us
  waiting for transfers between devices  232 us (34%)
  blocking collectives  147 us (22%)
  matrix products  102 us (15%)
  local copies, waits for them, and re-layouts  94.6 us (14%)
  other arithmetic  71 us (10%)
  between operations  22.4 us (3%)
    all_gather x1, waiting for transfers between devices, get_spans_here(): return lax.all_gather(tile_in, axis_name='mp').sum(axis=0)  76.9 us
    psum x1, waiting for transfers between devices, per_device(): lax.psum(attn_part.astype(jnp.bfloat16), 'mp').astype(jnp.float32)  63.4 us
    psum x1, waiting for transfers between devices, per_device(): lax.psum(second_part.astype(jnp.bfloat16), 'mp').astype(jnp.float32)  44.7 us
    all_gather x1, blocking collectives, per_device(): lax.all_gather(triple_weight.astype(bf16), 'dp', axis=1, tiled=True)  40.5 us
    psum x1, blocking collectives, per_device(): vectors = lax.psum((grad_norms, grad_paired, grad_hidden), 'dp')  37.6 us
    psum x1, blocking collectives, per_device(): total_square = lax.psum(local_square, ('dp', 'mp'))  36.9 us
    unnamed x122, local copies, waits for them, and re-layouts  33.4 us
    all_gather x1, blocking collectives, per_device(): lax.all_gather(outward_weight.astype(bf16), 'dp', axis=1, tiled=True)  31.8 us
  transfers between devices with their start and end apart: 10, of which 6 were waited for; matrix products, arithmetic and copies ran while one was open for 26% of the time, Pallas kernels for 0%

profile of v1, /device:TPU:0, one launch (start us, length us, event | category | flops | bytes accessed | tf_op | source)
XLA Modules:
  0.0 670.2 jit_solution(7695421517334138171)
XLA Ops:
  8.1 2.5 convert_reduce_fusion.2
  12.8 40.5 %all_gather.18 = bf16[3,768,192]{2,0,1:T(4,128)(2,1)} all-gather(bf16[3,96,192]{2,0,1:T(4,128)(2,1)S(1)} %copy.118), channel_id=1, replica_groups=mesh['dp'=8,'mp'=4] {'dp'}, dimensions={1}, use_global_device_ids=true | all-gather | bytes 995328 | tf_op jit(solution)/shard_map/all_gather | solution.py:82
  53.2 3.4 copy.119
  56.7 3.4 fusion.96
  61.1 2.0 fusion.107
  65.1 31.8 %all_gather.19 = bf16[192,768]{0,1:T(8,128)(2,1)S(1)} all-gather(bf16[192,96]{0,1:T(8,128)(2,1)} %copy.127), channel_id=1, replica_groups=mesh['dp'=8,'mp'=4] {'dp'}, dimensions={1}, use_global_device_ids=true | all-gather | bytes 331776 | tf_op jit(solution)/shard_map/all_gather | solution.py:83
  96.8 3.4 convert_element_type.132
  100.2 3.4 copy.123
  103.6 3.6 squeeze.4
  107.2 3.9 copy.120
  111.1 3.6 squeeze.10
  114.7 5.7 fusion.108
  121.4 2.1 copy-done.4
  124.5 2.2 copy.126
  126.7 3.5 reshape.145
  130.2 3.9 convolution_convert_fusion.2
  138.2 63.4 %all-reduce.5.cloned.1.call-done = bf16[2048,768]{1,0:T(8,128)(2,1)} async-done(((bf16[2048,768]{1,0:T(8,128)(2,1)}), bf16[2048,768]{1,0:T(8,128)(2,1)}) %all-reduce.5.cloned.1.call-update) | async-done | bytes 3145744 | tf_op jit(solution)/shard_map/psum | solution.py:117
  201.6 3.1 fusion.46
  204.7 1.8 multiply_reduce_fusion
  207.2 2.9 add_convert_fusion.1
  210.1 7.5 %fusion.111 = f32[2048,768]{1,0:T(8,128)} fusion(bf16[2048,768]{1,0:T(8,128)(2,1)} %add_convert_fusion.1, bf16[768,768]{1,0:T(8,128)(2,1)} %all-gather.5.cloned.1.call-done), kind=kOutput, calls=%fused_computation.161 | convolution fusion | flops 2415919104 | bytes 10616832 | tf_op jit(solution)/shard_map/dot_general | solution.py:121
  217.6 2.5 all-gather.7.cloned.1.call-done
  220.1 10.8 %convert_reduce_fusion.4 = (f32[768]{0:T(1024)}, bf16[2048,768]{1,0:T(8,128)(2,1)S(1)}, bf16[2048,768]{1,0:T(8,128)(2,1)}) fusion(f32[2048,768]{1,0:T(8,128)} %fusion.111, f32[768]{0:T(1024)} %param.45, bf16[2048,768]{1,0:T(8,128)(2,1)} %param.26, bf16[768,768]{0,1:T(8,128)(2,1)} %all-gather.7.cloned.1.call-done), kind=kOutput, calls=%fused_computation.46 | convolution fusion | flops 2455239936 | bytes 16914432 | tf_op jit(solution)/shard_map/td,fd->tf/dot_general | solution.py:129
  230.9 1.7 copy-done.53
  232.6 4.0 convolution_convert_fusion
  236.7 6.5 convolution_convert_fusion.1
  243.5 6.9 %fusion.112 = f32[768,768]{1,0:T(8,128)} fusion(bf16[2048,768]{1,0:T(8,128)(2,1)} %add_convert_fusion.1, bf16[2048,768]{1,0:T(8,128)(2,1)} %copy-done.53), kind=kOutput, calls=%fused_computation.162 | convolution fusion | flops 2415919104 | bytes 8650752 | tf_op jit(solution)/shard_map/td,tf->df/dot_general | solution.py:131
  250.5 6.9 %fusion.113 = f32[768,768]{0,1:T(8,128)} fusion(bf16[2048,768]{1,0:T(8,128)(2,1)} %get-tuple-element.165, bf16[2048,768]{1,0:T(8,128)(2,1)} %param.26), kind=kOutput, calls=%fused_computation.163 | convolution fusion | flops 2415919104 | bytes 8650752 | tf_op jit(solution)/shard_map/tf,td->fd/dot_general | solution.py:128
  259.0 44.7 %all-reduce.7.cloned.1.call-done = bf16[2048,768]{1,0:T(8,128)(2,1)} async-done(((bf16[2048,768]{1,0:T(8,128)(2,1)}), bf16[2048,768]{1,0:T(8,128)(2,1)}) %all-reduce.7.cloned.1.call-update) | async-done | bytes 3145744 | tf_op jit(solution)/shard_map/psum | solution.py:134
  303.8 6.3 fusion.30
  310.7 76.9 %all-gather.9.cloned.1.call-done = bf16[8192,768]{1,0:T(8,128)(2,1)} async-done(((bf16[2048,768]{1,0:T(8,128)(2,1)}), bf16[8192,768]{1,0:T(8,128)(2,1)}) %all-gather.9.cloned.1.call-update) | async-done | bytes 12582928 | tf_op jit(solution)/shard_map/all_gather | solution.py:75
  387.6 9.0 %reduce_sum.251 = bf16[2048,768]{1,0:T(8,128)(2,1)} reduce(bf16[4,2048,768]{2,1,0:T(8,128)(2,1)} %bitcast.78, bf16[]{:T(256)} %constant.36.clone.1), dimensions={0}, to_apply=%region_7.8 | reduce | flops 4718592 | bytes 15728642 | tf_op jit(solution)/shard_map/reduce_sum | solution.py:75
  396.6 9.3 %fusion.106 = (f32[768]{0:T(1024)}, f32[2048,768]{1,0:T(8,128)S(1)}, bf16[2048,768]{1,0:T(8,128)(2,1)}, f32[768]{0:T(1024)}) fusion(f32[2048]{0:T(1024)} %get-tuple-element.175, f32[2048]{0:T(1024)S(1)} %broadcast_multiply_fusion.4, f32[768]{0:T(1024)S(1)} %get-tuple-element.131, bf16[2048,768]{1,0:T(8,128)(2,1)} %all-reduce.5.cloned.1.call-done, ...), kind=kLoop, calls=%fused_computation.158 | loop fusion | flops 31455744 | bytes 25213952 | tf_op jit(solution)/shard_map/reduce_sum | solution.py:173
  405.9 2.7 copy-done.1
  408.6 2.1 convolution_convert_fusion.3
  410.7 3.4 reshape.146
  414.1 3.4 copy.128
  417.5 5.0 fusion.81
  422.6 8.0 %convert_reduce_fusion.6 = (f32[3,64]{1,0:T(4,128)S(1)}, bf16[32,64,3,64]{3,1,2,0:T(8,128)(2,1)}) fusion(bf16[32,64,3,64]{3,1,2,0:T(8,128)(2,1)} %copy.123, f32[32,3,64,64]{2,3,1,0:T(8,128)} %fusion.81, f32[32,3,64,64]{2,3,1,0:T(8,128)} %copy-done.3, f32[32,3,64]{2,1,0:T(4,128)S(1)} %copy-done.20), kind=kOutput, calls=%fused_computation.60 | convolution fusion | flops 54269824 | bytes 4743936 | tf_op jit(solution)/shard_map/rhqk,rkhd->rqhd/dot_general | solution.py:151
  430.5 3.2 copy.131
  433.7 3.7 stack.42
  437.5 10.1 %fusion.71 = bf16[32,64,3,64]{1,3,2,0:T(8,128)(2,1)} fusion(f32[32,3,64,64]{2,3,1,0:T(8,128)} %fusion.81, f32[32,3,64,64]{2,3,1,0:T(8,128)} %copy-done.3, f32[32,3,64]{2,1,0:T(4,128)S(1)} %copy-done.20, f32[32,64,3,64]{1,0,3,2:T(8,128)} %squeeze.10, f32[3,64]{1,0:T(4,128)S(1)} %copy-done.41), kind=kOutput, calls=%fused_computation.91 | convolution fusion | flops 54270016 | bytes 5530368 | tf_op jit(solution)/shard_map/rhqk,rqhd->rkhd/dot_general | solution.py:154
  447.5 4.3 convert_reduce_fusion.5
  451.9 5.1 fusion.78
  457.1 2.1 constant_dynamic-update-slice_fusion.2
  459.1 3.6 copy.133
  462.7 3.9 stack.43
  466.6 3.2 copy.135
  469.8 3.5 stack.44
  473.3 2.2 constant_dynamic-update-slice_fusion.1
  475.5 2.1 constant_dynamic-update-slice_fusion
  477.7 6.0 bitcast_convert_fusion
  484.4 5.2 fusion.65
  489.6 4.2 copy.149
  493.8 4.8 reshape.152
  499.5 1.8 copy.137
  501.3 1.8 copy.138
  506.7 12.8 %reduce-scatter.15.cloned.1.call-done = f32[96,192]{1,0:T(8,128)} async-done(((f32[768,192]{1,0:T(8,128)}), f32[96,192]{1,0:T(8,128)}) %reduce-scatter.15.cloned.1.call-update) | async-done | bytes 73744
  521.2 31.1 %all-reduce.9.cloned.1.call-done = bf16[2048,768]{1,0:T(8,128)(2,1)} async-done(((bf16[2048,768]{1,0:T(8,128)(2,1)}), bf16[2048,768]{1,0:T(8,128)(2,1)}) %all-reduce.9.cloned.1.call-update) | async-done | bytes 3145744 | tf_op jit(solution)/shard_map/psum | solution.py:163
  552.3 4.6 fusion.31
  557.0 37.6 %all-reduce = (f32[6,768]{1,0:T(8,128)S(1)}, f32[2,192]{1,0:T(2,128)S(1)}, f32[768]{0:T(1024)S(1)}) all-reduce(f32[6,768]{1,0:T(8,128)S(1)} %stack.52, f32[2,192]{1,0:T(2,128)S(1)} %pad_maximum_fusion, f32[768]{0:T(1024)S(1)} %copy-done.49), channel_id=1, replica_groups=mesh['dp'=8,'mp'=4] {'dp'}, use_global_device_ids=true, to_apply=%region_29.30 | all-reduce | flops 5760 | bytes 46080 | tf_op jit(solution)/shard_map/psum | solution.py:183
  599.6 1.9 reshape.153
  605.9 6.1 fusion.16
  612.1 36.9 %psum.55 = f32[]{:T(128)} all-reduce(f32[]{:T(128)S(6)} %add.292), channel_id=1, replica_groups=mesh['dp'=8,'mp'=4] {'dp','mp'}, use_global_device_ids=true, to_apply=%region_38.39 | all-reduce | flops 1 | bytes 8 | tf_op jit(solution)/shard_map/psum | solution.py:192
  (181 shorter events, 37.9 us)
Async XLA Ops:
  8.0 2.8 copy-start
  8.0 3.9 copy-start.27
  8.0 4.5 copy-start.10
  8.1 193.5 %all-reduce.5.cloned.1.call-start = ((), (), s32[]{:S(2)}) async-start(), calls=%async_computation.4 | async-start | bytes 6291456 | tf_op jit(solution)/shard_map/psum | solution.py:117
  10.9 45.8 %copy-start.22 = (f32[2048]{0:T(1024)}, f32[2048]{0:T(1024)S(1)}, u32[]{:S(2)}) copy-start(f32[2048]{0:T(1024)S(1)} %broadcast_multiply_fusion.5) | copy-start | bytes 24580
  12.0 48.1 %copy-start.28 = (f32[2048]{0:T(1024)}, f32[2048]{0:T(1024)S(1)}, u32[]{:S(2)}) copy-start(f32[2048]{0:T(1024)S(1)} %add_rsqrt_fusion.1) | copy-start | bytes 24580
  12.6 47.5 %copy-start.31 = (f32[768]{0:T(1024)}, f32[768]{0:T(1024)S(1)}, u32[]{:S(2)}) copy-start(f32[768]{0:T(1024)S(1)} %get-tuple-element.133) | copy-start | bytes 9220
  12.6 47.5 %copy-start.50 = (f32[768]{0:T(1024)}, f32[768]{0:T(1024)S(1)}, u32[]{:S(2)}) copy-start(f32[768]{0:T(1024)S(1)} %get-tuple-element.132) | copy-start | bytes 9220
  61.1 2.0 copy-start.46
  61.1 2.2 copy-start.14
  61.1 2.9 copy-start.30
  63.2 58.1 %copy-start.42 = (f32[3,64]{1,0:T(4,128)}, f32[3,64]{1,0:T(4,128)S(1)}, u32[]{:S(2)}) copy-start(f32[3,64]{1,0:T(4,128)S(1)} %add.262) | copy-start | bytes 2308
  63.3 51.4 %copy-start.40 = (f32[3,64]{1,0:T(4,128)}, f32[3,64]{1,0:T(4,128)S(1)}, u32[]{:S(2)}) copy-start(f32[3,64]{1,0:T(4,128)S(1)} %add.265) | copy-start | bytes 2308
  120.4 4.1 copy-start.3
  120.4 4.1 copy-start.13
  120.4 3.0 copy-start.4
  123.5 1.0 copy-start.21
  134.1 76.0 %all-gather.5.cloned.1.call-start = ((), (), s32[]{:S(2)}) async-start(), calls=%async_computation.5 | async-start | bytes 1327104 | tf_op jit(solution)/shard_map/all_gather | solution.py:84
  135.8 84.3 %all-gather.7.cloned.1.call-start = ((), (), s32[]{:S(2)}) async-start(), calls=%async_computation.6 | async-start | bytes 1327104 | tf_op jit(solution)/shard_map/all_gather | solution.py:85
  137.5 166.2 %all-reduce.7.cloned.1.call-start = ((), (), s32[]{:S(2)}) async-start(), calls=%async_computation.7 | async-start | bytes 6291456 | tf_op jit(solution)/shard_map/psum | solution.py:134
  201.6 3.2 copy-start.2
  204.7 2.4 copy-start.33
  206.5 0.6 copy-start.24
  220.1 12.6 %copy-start.52 = (bf16[768,768]{1,0:T(8,128)(2,1)S(1)}, bf16[768,768]{1,0:T(8,128)(2,1)}, u32[]{:S(2)}) copy-start(bf16[768,768]{1,0:T(8,128)(2,1)} %all-gather.5.cloned.1.call-done) | copy-start | bytes 3538948
  230.9 1.7 copy-start.53
  236.7 150.9 %all-gather.9.cloned.1.call-start = ((), (), s32[]{:S(2)}) async-start(), calls=%async_computation.11 | async-start | bytes 15728640 | tf_op jit(solution)/shard_map/all_gather | solution.py:75
  243.3 260.0 %reduce-scatter.9.cloned.1.call-start = ((), (), s32[]{:S(2)}) async-start(), calls=%async_computation.9 | async-start | bytes 2654208 | tf_op jit(solution)/shard_map/reduce_scatter | solution.py:180
  250.4 254.4 %reduce-scatter.11.cloned.1.call-start = ((), (), s32[]{:S(2)}) async-start(), calls=%async_computation.10 | async-start | bytes 2654208 | tf_op jit(solution)/shard_map/reduce_scatter | solution.py:181
  257.5 262.1 %reduce-scatter.15.cloned.1.call-start = ((), (), s32[]{:S(2)}) async-start(), calls=%async_computation.13 | async-start | bytes 884736
  405.9 2.7 copy-start.1
  410.7 6.8 %copy-start.43 = (f32[3,64]{1,0:T(4,128)S(1)}, f32[3,64]{1,0:T(4,128)}, u32[]{:S(2)}) copy-start(f32[3,64]{1,0:T(4,128)} %copy-done.42) | copy-start | bytes 2308
  417.5 5.1 copy-start.20
  430.5 6.9 %copy-start.41 = (f32[3,64]{1,0:T(4,128)S(1)}, f32[3,64]{1,0:T(4,128)}, u32[]{:S(2)}) copy-start(f32[3,64]{1,0:T(4,128)} %copy-done.40) | copy-start | bytes 2308
  447.5 4.3 copy-start.5
  457.0 95.3 %all-reduce.9.cloned.1.call-start = ((), (), s32[]{:S(2)}) async-start(), calls=%async_computation.8 | async-start | bytes 6291456 | tf_op jit(solution)/shard_map/psum | solution.py:163
  473.3 4.3 copy-start.12
  483.7 0.7 copy-start.23
  483.7 0.7 copy-start.29
  483.7 0.7 copy-start.32
  483.7 0.7 copy-start.51
  483.7 115.8 %reduce-scatter.13.cloned.1.call-start = ((), (), s32[]{:S(2)}) async-start(), calls=%async_computation.12 | async-start | bytes 2211840
  493.8 4.8 copy-start.11
  498.6 4.6 copy-start.35
  498.6 4.6 copy-start.34
  498.6 7.9 %copy-start.37 = (f32[768]{0:T(1024)S(1)}, f32[768]{0:T(1024)}, u32[]{:S(2)}) copy-start(f32[768]{0:T(1024)} %get-tuple-element.162) | copy-start | bytes 9220
  498.6 7.9 %copy-start.36 = (f32[768]{0:T(1024)S(1)}, f32[768]{0:T(1024)}, u32[]{:S(2)}) copy-start(f32[768]{0:T(1024)} %get-tuple-element.168) | copy-start | bytes 9220
  521.2 35.8 %copy-start.49 = (f32[768]{0:T(1024)S(1)}, f32[768]{0:T(1024)}, u32[]{:S(2)}) copy-start(f32[768]{0:T(1024)} %get-tuple-element.160) | copy-start | bytes 9220
  594.6 6.9 %copy-start.26 = (f32[6,768]{1,0:T(8,128)}, f32[6,768]{1,0:T(8,128)S(1)}, u32[]{:S(2)}) copy-start(f32[6,768]{1,0:T(8,128)S(1)} %get-tuple-element.136) | copy-start | bytes 55300
  594.6 6.9 %copy-start.38 = (f32[768]{0:T(1024)}, f32[768]{0:T(1024)S(1)}, u32[]{:S(2)}) copy-start(f32[768]{0:T(1024)S(1)} %get-tuple-element.138) | copy-start | bytes 9220
  594.6 6.8 %copy-start.44 = (f32[2,192]{1,0:T(2,128)}, f32[2,192]{1,0:T(2,128)S(1)}, u32[]{:S(2)}) copy-start(f32[2,192]{1,0:T(2,128)S(1)} %get-tuple-element.137) | copy-start | bytes 4612
  612.0 41.8 %copy-start.45 = (f32[2,192]{1,0:T(2,128)S(1)}, f32[2,192]{1,0:T(2,128)}, u32[]{:S(2)}) copy-start(f32[2,192]{1,0:T(2,128)} %copy-done.44) | copy-start | bytes 4612
  612.0 41.8 %copy-start.47 = (f32[2,192]{1,0:T(2,128)S(1)}, f32[2,192]{1,0:T(2,128)}, u32[]{:S(2)}) copy-start(f32[2,192]{1,0:T(2,128)} %param.42) | copy-start | bytes 4612
  612.0 43.2 %copy-start.39 = (f32[768]{0:T(1024)S(1)}, f32[768]{0:T(1024)}, u32[]{:S(2)}) copy-start(f32[768]{0:T(1024)} %copy-done.38) | copy-start | bytes 9220
  612.0 43.1 %copy-start.48 = (f32[768]{0:T(1024)S(1)}, f32[768]{0:T(1024)}, u32[]{:S(2)}) copy-start(f32[768]{0:T(1024)} %param.45) | copy-start | bytes 9220
  612.0 45.9 %copy-start.15 = (f32[192,96]{1,0:T(8,128)S(1)}, f32[192,96]{1,0:T(8,128)}, u32[]{:S(2)}) copy-start(f32[192,96]{1,0:T(8,128)} %param.30) | copy-start | bytes 221188
  612.0 45.9 %copy-start.25 = (f32[192,96]{1,0:T(8,128)S(1)}, f32[192,96]{1,0:T(8,128)}, u32[]{:S(2)}) copy-start(f32[192,96]{1,0:T(8,128)} %param.32) | copy-start | bytes 221188
  612.0 47.5 %copy-start.6 = (f32[96,768]{1,0:T(8,128)S(1)}, f32[96,768]{1,0:T(8,128)}, u32[]{:S(2)}) copy-start(f32[96,768]{1,0:T(8,128)} %param.33) | copy-start | bytes 884740
  612.1 47.5 %copy-start.8 = (f32[96,768]{1,0:T(8,128)S(1)}, f32[96,768]{1,0:T(8,128)}, u32[]{:S(2)}) copy-start(f32[96,768]{1,0:T(8,128)} %reduce-scatter.9.cloned.1.call-done) | copy-start | bytes 884740
  612.1 47.5 %copy-start.16 = (f32[96,768]{1,0:T(8,128)S(1)}, f32[96,768]{1,0:T(8,128)}, u32[]{:S(2)}) copy-start(f32[96,768]{1,0:T(8,128)} %param.35) | copy-start | bytes 884740
  612.1 47.5 %copy-start.17 = (f32[96,768]{1,0:T(8,128)S(1)}, f32[96,768]{1,0:T(8,128)}, u32[]{:S(2)}) copy-start(f32[96,768]{1,0:T(8,128)} %param.34) | copy-start | bytes 884740
  649.7 10.9 %copy-start.7 = (f32[768,96]{0,1:T(8,128)S(1)}, f32[768,96]{0,1:T(8,128)}, u32[]{:S(2)}) copy-start(f32[768,96]{0,1:T(8,128)} %param.36) | copy-start | bytes 884740
  649.7 10.9 %copy-start.9 = (f32[768,96]{0,1:T(8,128)S(1)}, f32[768,96]{0,1:T(8,128)}, u32[]{:S(2)}) copy-start(f32[768,96]{0,1:T(8,128)} %reduce-scatter.11.cloned.1.call-done) | copy-start | bytes 884740
  649.7 10.9 %copy-start.18 = (f32[768,96]{0,1:T(8,128)S(1)}, f32[768,96]{0,1:T(8,128)}, u32[]{:S(2)}) copy-start(f32[768,96]{0,1:T(8,128)} %param.38) | copy-start | bytes 884740
  651.2 9.4 %copy-start.19 = (f32[768,96]{0,1:T(8,128)S(1)}, f32[768,96]{0,1:T(8,128)}, u32[]{:S(2)}) copy-start(f32[768,96]{0,1:T(8,128)} %param.37) | copy-start | bytes 884740
Sparse Core Ops, SparseCore 0:
  134.2 67.3 all-reduce.4
  236.8 66.9 all-reduce.6
  305.3 82.2 all-gather.8
  483.8 68.4 all-reduce.8
Sparse Core Ops, SparseCore 1:
  137.3 40.2 all-gather.4
  180.2 39.8 all-gather.6
  250.5 67.7 reduce-scatter.8
  321.8 68.1 reduce-scatter.10
  457.1 62.4 reduce-scatter.14
  523.5 66.5 reduce-scatter.12
